TPU v7x, 32 devices: a whole 2x2x4 slice. The times are simulated.
32 devices in a mesh: row: 8 (over y, x, core), section: 4 (over z).
Axes of the slice: x: 2, y: 2, z: 4, core: 2. Of those that a mesh axis runs over, the one named last changes fastest.
Arguments:
- features: bfloat16 [8192, 256], P('row'), may hold values from -6 to 6
- weight: bfloat16 [256, 256], replicated, may hold values from -0.375 to 0.375
- cotangent: bfloat16 [8192, 256], P('row'), may hold values from -0.0625 to 0.0625
- counts: int32 [64, 16, 128, 128], P('row', 'section'), may hold values from 0 to 3, as said below
- columns: int32 [64, 16], P('row', 'section'), may hold values from 0 to 63, as said below
- live_slots: int32 [64, 4], P('row', 'section'), may hold values from 1 to 4, as said below
Outputs:
- output: bfloat16 [8192, 256], P('row')
- grad_weight: float32 [256, 256], replicated
Inputs may be any that keep to these rules, and one draw needn't show every extreme that they name: `columns`: every entry in a slot of section index s names a node block g with (g // 8) % 4 == s; the 4 slots of one row of blocks and one section index name distinct column blocks. Slots at k >= live_slots[b, s] are ignored; the value 4 occurs at every section index in every draw. `counts`: most entries are zero.
All inputs are finite; a program needn't handle non-finite values.
Results may differ from a plain program's by a relative error of at most 0.0055.
Values may be sent and summed in bfloat16 or wider, within the bound.
A program may use at most 64 MiB of HBM per device.

v0:
```python
import jax
import jax.numpy as jnp
from jax import lax
from jax.sharding import PartitionSpec as P


def per_device(features, weight, cotangent, counts, columns, live_slots):
    row_count = features.shape[0]
    feat_width = features.shape[1]
    block_count = columns.shape[0]
    slot_count = columns.shape[1]
    block_size = counts.shape[2]
    section_index = lax.axis_index("section")
    section_count = lax.axis_size("section")
    owner_count = lax.axis_size("row") // section_count
    everything = lax.all_gather(features, "row", axis=0, tiled=True)
    grouped = everything.reshape(owner_count, section_count, row_count, feat_width)
    window = lax.dynamic_index_in_dim(grouped, section_index, 1, keepdims=False)
    window = window.reshape(owner_count * block_count, block_size, feat_width)
    local_cols = columns // block_count // section_count * block_count + columns % block_count
    slot_used = jnp.arange(slot_count, dtype=jnp.int32)[None, :] < live_slots
    masked = jnp.where(slot_used[:, :, None, None], counts, 0)
    degree = jnp.sum(masked, axis=(1, 3)).astype(jnp.float32).reshape(row_count)
    edge_mats = masked.astype(jnp.bfloat16)
    picked = window[local_cols]
    partial_value = jnp.einsum(
        "rkij,rkjf->rif", edge_mats, picked, preferred_element_type=jnp.float32
    )
    partial_value = partial_value.reshape(row_count, feat_width)
    summed, degree_all = lax.psum((partial_value, degree), "section")
    aggregate = (summed * lax.rsqrt(1.0 + degree_all)[:, None]).astype(jnp.bfloat16)
    pre_act = jnp.dot(aggregate, weight, preferred_element_type=jnp.float32)
    gate_value = jax.nn.sigmoid(pre_act)
    output = (pre_act * gate_value).astype(jnp.bfloat16)
    grad_pre = (
        cotangent.astype(jnp.float32) * gate_value * (1.0 + pre_act * (1.0 - gate_value))
    ).astype(jnp.bfloat16)
    grad_local = lax.dot_general(
        aggregate, grad_pre, (((0,), (0,)), ((), ())), preferred_element_type=jnp.float32
    )
    grad_weight = lax.psum(grad_local, "row")
    return (output, grad_weight)


def solution(mesh):
    in_specs = (
        P("row", None),
        P(),
        P("row", None),
        P("row", "section", None, None),
        P("row", "section"),
        P("row", "section"),
    )
    out_specs = (P("row", None), P())
    return jax.shard_map(
        per_device, mesh=mesh, in_specs=in_specs, out_specs=out_specs, check_vma=False
    )
```

profile of v0, /device:TPU:0, one launch (start us, length us, event | category | flops | bytes accessed | tf_op | source)
XLA Modules:
  0.0 172.0 jit_solution(4953633193396426414)
XLA Ops:
  7.2 0.0 copy-start
  7.2 0.0 all-gather.2.cloned.1.call-start
  7.2 0.7 all-gather.2.cloned.1.call-update
  7.9 0.0 all-reduce.3.cloned.1.call-start
  8.0 0.7 compare_select_fusion
  8.7 0.1 copy.9
  8.8 0.1 reshape.45
  8.8 0.7 iota_compare_fusion
  9.6 39.8 %all-gather.2.cloned.1.call-done = bf16[8192,256]{1,0:T(8,128)(2,1)} async-done(((bf16[1024,256]{1,0:T(8,128)(2,1)}), bf16[8192,256]{1,0:T(8,128)(2,1)}) %all-gather.2.cloned.1.call-update) | async-done | bytes 4194320 | tf_op jit(solution)/shard_map/all_gather | solution.py:16
  49.4 1.3 constant_dynamic-slice_fusion
  50.6 0.7 gather_fusion
  51.3 3.2 %fusion = f32[8,128,256,1]{2,1,3,0:T(8,128)} fusion(bf16[8,4,128,256]{3,2,1,0:T(8,128)(2,1)S(1)} %bitcast.13, s32[8,4,128,128]{3,2,1,0:T(8,128)} %param.9, pred[8,4]{1,0:T(8,128)(4,1)S(1)} %iota_compare_fusion), kind=kOutput, calls=%fused_computation.3 | convolution fusion | flops 269484032 | bytes 5242912 | tf_op jit(solution)/shard_map/rkij,rkjf->rif/dot_general | solution.py:26
  54.5 0.0 all-reduce.3.cloned.1.call-update
  54.5 0.0 all-reduce.5.cloned.1.call-start
  54.6 1.9 %select_reduce_fusion = s32[8,128]{1,0:T(8,128)S(1)} fusion(s32[8,4,128,128]{3,2,1,0:T(8,128)} %param.9, pred[8,4]{1,0:T(8,128)(4,1)S(1)} %iota_compare_fusion), kind=kLoop, calls=%fused_computation.1 | loop fusion | flops 1047552 | bytes 2101280 | tf_op jit(solution)/shard_map/reduce_sum | solution.py:23
  56.5 11.9 %psum.22 = f32[1024]{0:T(1024)S(1)} all-reduce(f32[1024]{0:T(1024)S(1)} %convert_bitcast_fusion), channel_id=1, replica_groups=mesh['row'=8,'section'=4] {'section'}, use_global_device_ids=true, to_apply=%region_2.3 | all-reduce | flops 1024 | bytes 8192 | tf_op jit(solution)/shard_map/psum | solution.py:30
  68.5 0.0 copy-start.2
  68.5 38.2 %all-reduce.3.cloned.1.call-done = f32[1024,256]{1,0:T(8,128)} async-done(((f32[1024,256]{1,0:T(8,128)}), f32[1024,256]{1,0:T(8,128)}) %all-reduce.3.cloned.1.call-update) | async-done | bytes 1048592 | tf_op jit(solution)/shard_map/psum | solution.py:30
  106.6 0.0 copy-done
  106.6 0.0 copy-start.1
  106.6 2.6 %multiply_convert_fusion.1 = (bf16[1024,256]{1,0:T(8,128)(2,1)}, f32[1024,256]{1,0:T(8,128)S(1)}) fusion(bf16[256,256]{1,0:T(8,128)(2,1)S(1)} %copy-done, f32[1024,256]{1,0:T(8,128)} %all-reduce.3.cloned.1.call-done, f32[1024]{0:T(1024)S(1)} %add_rsqrt_fusion), kind=kOutput, calls=%fused_computation.5 | convolution fusion | flops 136052736 | bytes 2756608 | tf_op jit(solution)/shard_map/dot_general | solution.py:32
  109.2 0.0 copy-done.2
  109.2 0.0 copy-done.1
  109.2 1.5 fusion.3
  110.7 0.0 all-reduce.5.cloned.1.call-update
  110.7 53.1 %all-reduce.5.cloned.1.call-done = f32[256,256]{1,0:T(8,128)} async-done(((f32[256,256]{1,0:T(8,128)}), f32[256,256]{1,0:T(8,128)}) %all-reduce.5.cloned.1.call-update) | async-done | bytes 262160 | tf_op jit(solution)/shard_map/psum | solution.py:41
  163.8 1.7 copy.13
  (3 shorter events, 0.0 us)
Async XLA Ops:
  7.2 99.5 %copy-start = (bf16[256,256]{1,0:T(8,128)(2,1)S(1)}, bf16[256,256]{1,0:T(8,128)(2,1)}, u32[]{:S(2)}) copy-start(bf16[256,256]{1,0:T(8,128)(2,1)} %param.7) | copy-start | bytes 393220
  7.2 42.2 %all-gather.2.cloned.1.call-start = ((), (), s32[]{:S(2)}) async-start(), calls=%async_computation | async-start | bytes 4718592 | tf_op jit(solution)/shard_map/all_gather | solution.py:16
  7.9 98.7 %all-reduce.3.cloned.1.call-start = ((), (), s32[]{:S(2)}) async-start(), calls=%async_computation.1 | async-start | bytes 2097152 | tf_op jit(solution)/shard_map/psum | solution.py:30
  54.5 109.3 %all-reduce.5.cloned.1.call-start = ((), (), s32[]{:S(2)}) async-start(), calls=%async_computation.2 | async-start | bytes 524288 | tf_op jit(solution)/shard_map/psum | solution.py:41
  68.5 40.8 %copy-start.2 = (bf16[1024,256]{1,0:T(8,128)(2,1)S(1)}, bf16[1024,256]{1,0:T(8,128)(2,1)}, u32[]{:S(2)}) copy-start(bf16[1024,256]{1,0:T(8,128)(2,1)} %param.8) | copy-start | bytes 1572868
  106.6 2.6 %copy-start.1 = (f32[1024,256]{1,0:T(8,128)S(1)}, f32[1024,256]{1,0:T(8,128)}, u32[]{:S(2)}) copy-start(f32[1024,256]{1,0:T(8,128)} %all-reduce.3.cloned.1.call-done) | copy-start | bytes 3145732
Sparse Core Ops, SparseCore 0:
  9.9 39.4 all-gather.1
  54.7 51.9 all-reduce.2
  110.8 52.9 all-reduce.4
where the time goes:
time: 172 us
  waiting for transfers between devices  132 us (77%)
  between operations  13.8 us (8%)
  blocking collectives  11.9 us (7%)
  matrix products  7.25 us (4%)
  local copies, waits for them, and re-layouts  3.82 us (2%)
  other arithmetic  3.35 us (2%)
    psum x1, waiting for transfers between devices, per_device(): grad_weight = lax.psum(grad_local, 'row')  53.1 us
    all_gather x1, waiting for transfers between devices, per_device(): everything = lax.all_gather(features, 'row', axis=0, tiled=True)  39.8 us
    psum x1, waiting for transfers between devices, per_device(): summed, degree_all = lax.psum((partial_value, degree), 'section')  38.2 us
    psum x1, blocking collectives, per_device(): summed, degree_all = lax.psum((partial_value, degree), 'section')  11.9 us
  transfers between devices with their start and end apart: 3, of which 3 were waited for; matrix products, arithmetic and copies ran while one was open for 2% of the time, Pallas kernels for 0%

commit v1 on v0

--- a/solution.py
+++ b/solution.py
@@ -38,7 +38,11 @@
     grad_local = lax.dot_general(
         aggregate, grad_pre, (((0,), (0,)), ((), ())), preferred_element_type=jnp.float32
     )
-    grad_weight = lax.psum(grad_local, "row")
+    grad_weight = grad_local
+    for hop in (1, 2, 4):
+        grad_weight = grad_weight + lax.ppermute(
+            grad_weight, "row", [(dev, dev ^ hop) for dev in range(8)]
+        )
     return (output, grad_weight)
 
 

time: 172 us -> 136 us (0.79)
  waiting for transfers between devices: 132 us -> 93.1 us
  starting transfers between devices: 0.12 us -> 3.25 us
    psum x1 -> x0, waiting for transfers between devices: 53.1 us -> none  [per_device(): grad_weight = lax.psum(grad_local, 'row')]
    ppermute x0 -> x3, waiting for transfers between devices: none -> 14.4 us  [per_device(): lax.ppermute(grad_weight, 'row', [(dev, dev ^ hop) for dev in range(8)])]
    ppermute x0 -> x3, starting transfers between devices: none -> 3.18 us  [per_device(): lax.ppermute(grad_weight, 'row', [(dev, dev ^ hop) for dev in range(8)])]
  transfers between devices with their start and end apart: 3 -> 5, of which waited for: 3 -> 5; matrix products, arithmetic and copies ran while one was open for 2% -> 3% of each run, Pallas kernels for 0% -> 0%
where the time goes in v1:
time: 136 us; the launch traced here: 135 us
  waiting for transfers between devices  93.1 us (68%)
  between operations  14.1 us (10%)
  blocking collectives  12 us (9%)
  matrix products  6.52 us (5%)
  other arithmetic  4.15 us (3%)
  starting transfers between devices  3.25 us (2%)
  local copies, waits for them, and re-layouts  2.16 us (2%)
    all_gather x1, waiting for transfers between devices, per_device(): everything = lax.all_gather(features, 'row', axis=0, tiled=True)  39.8 us
    psum x1, waiting for transfers between devices, per_device(): summed, degree_all = lax.psum((partial_value, degree), 'section')  38.2 us
    ppermute x3, waiting for transfers between devices, per_device(): lax.ppermute(grad_weight, 'row', [(dev, dev ^ hop) for dev in range(8)])  14.4 us
    psum x1, blocking collectives, per_device(): summed, degree_all = lax.psum((partial_value, degree), 'section')  12 us
    ppermute x3, starting transfers between devices, per_device(): lax.ppermute(grad_weight, 'row', [(dev, dev ^ hop) for dev in range(8)])  3.18 us
    dot_general x1, matrix products, per_device(): jnp.einsum('rkij,rkjf->rif', edge_mats, picked, preferred_element_type=jn...  3.16 us
  transfers between devices with their start and end apart: 5, of which 5 were waited for; matrix products, arithmetic and copies ran while one was open for 3% of the time, Pallas kernels for 0%

profile of v1, /device:TPU:0, one launch (start us, length us, event | category | flops | bytes accessed | tf_op | source)
XLA Modules:
  0.0 135.2 jit_solution(17042718334168374081)
XLA Ops:
  7.2 0.0 copy-start
  7.2 0.0 all-gather.2.cloned.1.call-start
  7.2 0.7 all-gather.2.cloned.1.call-update
  7.9 0.0 all-reduce.2.cloned.1.call-start
  8.0 0.7 compare_select_fusion
  8.7 0.1 copy.9
  8.8 0.1 reshape.45
  8.8 0.7 iota_compare_fusion
  9.6 39.8 %all-gather.2.cloned.1.call-done = bf16[8192,256]{1,0:T(8,128)(2,1)} async-done(((bf16[1024,256]{1,0:T(8,128)(2,1)}), bf16[8192,256]{1,0:T(8,128)(2,1)}) %all-gather.2.cloned.1.call-update) | async-done | bytes 4194320 | tf_op jit(solution)/shard_map/all_gather | solution.py:16
  49.4 1.3 constant_dynamic-slice_fusion
  50.6 0.7 gather_fusion
  51.3 3.2 %fusion = f32[8,128,256,1]{2,1,3,0:T(8,128)} fusion(bf16[8,4,128,256]{3,2,1,0:T(8,128)(2,1)S(1)} %bitcast.13, s32[8,4,128,128]{3,2,1,0:T(8,128)} %param.9, pred[8,4]{1,0:T(8,128)(4,1)S(1)} %iota_compare_fusion), kind=kOutput, calls=%fused_computation.3 | convolution fusion | flops 269484032 | bytes 5242912 | tf_op jit(solution)/shard_map/rkij,rkjf->rif/dot_general | solution.py:26
  54.5 0.0 all-reduce.2.cloned.1.call-update
  54.5 1.9 %select_reduce_fusion = s32[8,128]{1,0:T(8,128)S(1)} fusion(s32[8,4,128,128]{3,2,1,0:T(8,128)} %param.9, pred[8,4]{1,0:T(8,128)(4,1)S(1)} %iota_compare_fusion), kind=kLoop, calls=%fused_computation.1 | loop fusion | flops 1047552 | bytes 2101280 | tf_op jit(solution)/shard_map/reduce_sum | solution.py:23
  56.4 12.0 %psum.15 = f32[1024]{0:T(1024)S(1)} all-reduce(f32[1024]{0:T(1024)S(1)} %convert_bitcast_fusion), channel_id=1, replica_groups=mesh['row'=8,'section'=4] {'section'}, use_global_device_ids=true, to_apply=%region_2.3 | all-reduce | flops 1024 | bytes 8192 | tf_op jit(solution)/shard_map/psum | solution.py:30
  68.5 0.0 copy-start.2
  68.5 38.2 %all-reduce.2.cloned.1.call-done = f32[1024,256]{1,0:T(8,128)} async-done(((f32[1024,256]{1,0:T(8,128)}), f32[1024,256]{1,0:T(8,128)}) %all-reduce.2.cloned.1.call-update) | async-done | bytes 1048592 | tf_op jit(solution)/shard_map/psum | solution.py:30
  106.6 0.0 copy-done
  106.6 0.0 copy-start.1
  106.6 2.6 %multiply_convert_fusion.1 = (bf16[1024,256]{1,0:T(8,128)(2,1)}, f32[1024,256]{1,0:T(8,128)S(1)}) fusion(bf16[256,256]{1,0:T(8,128)(2,1)S(1)} %copy-done, f32[1024,256]{1,0:T(8,128)} %all-reduce.2.cloned.1.call-done, f32[1024]{0:T(1024)S(1)} %add_rsqrt_fusion), kind=kOutput, calls=%fused_computation.5 | convolution fusion | flops 136052736 | bytes 2756608 | tf_op jit(solution)/shard_map/dot_general | solution.py:32
  109.2 0.0 copy-done.2
  109.2 0.0 copy-done.1
  109.2 0.7 fusion.3
  110.0 0.1 collective-permute-start
  110.1 1.5 %collective-permute-done = f32[256,256]{1,0:T(8,128)S(1)} collective-permute-done((f32[256,256]{1,0:T(8,128)S(1)}, f32[256,256]{1,0:T(8,128)S(1)}, u32[]{:S(2)}, u32[]{:S(2)}) %collective-permute-start) | collective-permute-done | bytes 262176 | tf_op jit(solution)/shard_map/ppermute | solution.py:43
  111.6 1.5 %collective-permute-start.1 = (f32[256,256]{1,0:T(8,128)S(1)}, f32[256,256]{1,0:T(8,128)S(1)}, u32[]{:S(2)}, u32[]{:S(2)}) collective-permute-start(f32[256,256]{1,0:T(8,128)S(1)} %add.55), channel_id=1, source_target_pairs={{0,8},{4,12},{8,0},{12,4},{16,24},{20,28},{24,16},{28,20},{1,9},{5... | collective-permute-start | bytes 786440 | tf_op jit(solution)/shard_map/ppermute | solution.py:43
  113.2 6.9 %collective-permute-done.1 = f32[256,256]{1,0:T(8,128)S(1)} collective-permute-done((f32[256,256]{1,0:T(8,128)S(1)}, f32[256,256]{1,0:T(8,128)S(1)}, u32[]{:S(2)}, u32[]{:S(2)}) %collective-permute-start.1) | collective-permute-done | bytes 262176 | tf_op jit(solution)/shard_map/ppermute | solution.py:43
  120.1 1.5 %collective-permute-start.2 = (f32[256,256]{1,0:T(8,128)S(1)}, f32[256,256]{1,0:T(8,128)S(1)}, u32[]{:S(2)}, u32[]{:S(2)}) collective-permute-start(f32[256,256]{1,0:T(8,128)S(1)} %add.56), channel_id=1, source_target_pairs={{0,16},{4,20},{8,24},{12,28},{16,0},{20,4},{24,8},{28,12},{1,17},{... | collective-permute-start | bytes 786440 | tf_op jit(solution)/shard_map/ppermute | solution.py:43
  121.6 6.0 %collective-permute-done.2 = f32[256,256]{1,0:T(8,128)S(1)} collective-permute-done((f32[256,256]{1,0:T(8,128)S(1)}, f32[256,256]{1,0:T(8,128)S(1)}, u32[]{:S(2)}, u32[]{:S(2)}) %collective-permute-start.2) | collective-permute-done | bytes 262176 | tf_op jit(solution)/shard_map/ppermute | solution.py:43
  127.7 0.7 add.57
  (5 shorter events, 0.1 us)
Async XLA Ops:
  7.2 99.4 %copy-start = (bf16[256,256]{1,0:T(8,128)(2,1)S(1)}, bf16[256,256]{1,0:T(8,128)(2,1)}, u32[]{:S(2)}) copy-start(bf16[256,256]{1,0:T(8,128)(2,1)} %param.7) | copy-start | bytes 393220
  7.2 42.2 %all-gather.2.cloned.1.call-start = ((), (), s32[]{:S(2)}) async-start(), calls=%async_computation | async-start | bytes 4718592 | tf_op jit(solution)/shard_map/all_gather | solution.py:16
  7.9 98.7 %all-reduce.2.cloned.1.call-start = ((), (), s32[]{:S(2)}) async-start(), calls=%async_computation.1 | async-start | bytes 2097152 | tf_op jit(solution)/shard_map/psum | solution.py:30
  68.5 40.8 %copy-start.2 = (bf16[1024,256]{1,0:T(8,128)(2,1)S(1)}, bf16[1024,256]{1,0:T(8,128)(2,1)}, u32[]{:S(2)}) copy-start(bf16[1024,256]{1,0:T(8,128)(2,1)} %param.8) | copy-start | bytes 1572868
  106.6 2.6 %copy-start.1 = (f32[1024,256]{1,0:T(8,128)S(1)}, f32[1024,256]{1,0:T(8,128)}, u32[]{:S(2)}) copy-start(f32[1024,256]{1,0:T(8,128)} %all-reduce.2.cloned.1.call-done) | copy-start | bytes 3145732
  110.0 1.6 %collective-permute-start = (f32[256,256]{1,0:T(8,128)S(1)}, f32[256,256]{1,0:T(8,128)S(1)}, u32[]{:S(2)}, u32[]{:S(2)}) collective-permute-start(f32[256,256]{1,0:T(8,128)S(1)} %fusion.3), channel_id=1, source_target_pairs={{0,4},{4,0},{8,12},{12,8},{16,20},{20,16},{24,28},{28,24},{1,5},{5... | collective-permute-start | bytes 786440 | tf_op jit(solution)/shard_map/ppermute | solution.py:43
  111.6 8.4 %collective-permute-start.1 = (f32[256,256]{1,0:T(8,128)S(1)}, f32[256,256]{1,0:T(8,128)S(1)}, u32[]{:S(2)}, u32[]{:S(2)}) collective-permute-start(f32[256,256]{1,0:T(8,128)S(1)} %add.55), channel_id=1, source_target_pairs={{0,8},{4,12},{8,0},{12,4},{16,24},{20,28},{24,16},{28,20},{1,9},{5... | collective-permute-start | bytes 786440 | tf_op jit(solution)/shard_map/ppermute | solution.py:43
  120.1 7.6 %collective-permute-start.2 = (f32[256,256]{1,0:T(8,128)S(1)}, f32[256,256]{1,0:T(8,128)S(1)}, u32[]{:S(2)}, u32[]{:S(2)}) collective-permute-start(f32[256,256]{1,0:T(8,128)S(1)} %add.56), channel_id=1, source_target_pairs={{0,16},{4,20},{8,24},{12,28},{16,0},{20,4},{24,8},{28,12},{1,17},{... | collective-permute-start | bytes 786440 | tf_op jit(solution)/shard_map/ppermute | solution.py:43
Sparse Core Ops, SparseCore 0:
  9.9 39.4 all-gather.1
  54.6 51.9 all-reduce.1
